TPU v7x, 512 devices: a whole 4x4x16 slice. The times are simulated.
512 devices in a mesh: pairs: 64 (over x, z), grp: 8 (over y, core).
Axes of the slice: x: 4, y: 4, z: 16, core: 2. Of those that a mesh axis runs over, the one named last changes fastest.
Arguments:
- spectra: bfloat16 [8192, 1, 2048], P(('pairs', 'grp')), as said below
- row_station: int32 [8192], P(('pairs', 'grp')), may hold values from 0 to 4095, as said below
- row_window: int32 [8192], P(('pairs', 'grp')), may hold values from 0 to 1, as said below
- station_owner: int32 [4096], replicated, may hold values from 0 to 511, as said below
- tile_stations: int32 [64, 384], replicated, may hold values from 0 to 4095, as said below
- pair_index: int32 [64, 8, 2, 48], P('pairs', 'grp'), may hold values from 0 to 383
Outputs:
- correlation: float32 [64, 8, 48, 2001], P('pairs', 'grp')
Inputs may be any that keep to these rules, and one draw needn't show every extreme that they name: `row_station`: every station's 2 windows lie on the device that station_owner names, one row each; every device holds 8 stations. `row_window`: A device's rows of one station carry each window number once. `station_owner`: devices are numbered by pairs index times the size of grp plus grp index. `tile_stations`: A group's list holds distinct stations on distinct devices; exactly 48 of them lie on devices of each grp index. `spectra`: real parts of the 1024 bins, then their imaginary parts.
All inputs are finite; a program needn't handle non-finite values.
Results may differ from a plain program's by a relative error of at most 0.0056.
Values may be sent and summed in bfloat16 or wider, within the bound.
A program may use at most 64 MiB of HBM per device.

v0:
```python
import math
import jax
import jax.numpy as jnp
from jax import lax
from jax.sharding import PartitionSpec as P

W = 2
NSEG = 1
NFFT = 2048
BAND = 128
MAXLAG = 1000
LAGS = 2001
freq_block_max = 512
power_eps = 1e-06


def whiten_rows(spectra, band_width):
    half_bins = spectra.shape[-1] // 2
    leading = spectra.shape[:-1]
    values = spectra.astype(jnp.float32).reshape(leading + (2, half_bins // band_width, band_width))
    band_power = jnp.mean(jnp.sum(values * values, axis=-3), axis=-1)
    scaling = lax.rsqrt(band_power + power_eps)
    whitened = values * scaling[..., None, :, None]
    return whitened.reshape(spectra.shape).astype(jnp.bfloat16)


def lag_table(offset, bin_count):
    freq_index = (offset + jnp.arange(bin_count, dtype=jnp.int32))[:, None]
    lag_shift = (jnp.arange(LAGS, dtype=jnp.int32) + (NFFT - MAXLAG))[None, :]
    angles = (freq_index * lag_shift % NFFT).astype(jnp.float32) * (2.0 * math.pi / NFFT)
    return jnp.concatenate([jnp.cos(angles), -jnp.sin(angles)], axis=0).astype(jnp.bfloat16)


def cross_block(source_rows, first_rows, second_rows, offset, bin_count):
    half_bins = source_rows.shape[-1] // 2
    real_part = source_rows[:, :, offset : offset + bin_count]
    imag_part = source_rows[:, :, half_bins + offset : half_bins + offset + bin_count]
    real_a = real_part[first_rows].astype(jnp.float32)
    imag_a = imag_part[first_rows].astype(jnp.float32)
    real_b = real_part[second_rows].astype(jnp.float32)
    imag_b = imag_part[second_rows].astype(jnp.float32)
    cross_real = jnp.sum(real_a * real_b + imag_a * imag_b, axis=(1, 2))
    cross_imag = jnp.sum(imag_a * real_b - real_a * imag_b, axis=(1, 2))
    return jnp.concatenate([cross_real, cross_imag], axis=1).astype(jnp.bfloat16)


def correlate(source_rows, first_rows, second_rows):
    half_bins = NFFT // 2
    block_size = min(freq_block_max, half_bins)
    running = jnp.zeros((first_rows.shape[0], LAGS), jnp.float32)
    for offset in range(0, half_bins, block_size):
        cross_terms = cross_block(source_rows, first_rows, second_rows, offset, block_size)
        running = running + jnp.dot(
            cross_terms, lag_table(offset, block_size), preferred_element_type=jnp.float32
        )
    return running * (1.0 / math.sqrt(half_bins * W * NSEG))


def on_device(spectra, row_station, row_window, station_owner, tile_stations, pair_index):
    group_count = lax.axis_size("grp")
    pair_groups = lax.axis_size("pairs")
    my_pair = lax.axis_index("pairs")
    local_count = spectra.shape[0]
    row_tail = spectra.shape[1:]
    window_ids = jnp.arange(W, dtype=jnp.int32)
    local_ids = jnp.arange(local_count, dtype=jnp.int32)
    zero_value = jnp.zeros((), jnp.bfloat16)
    whitened = whiten_rows(spectra, BAND)
    my_tile = lax.dynamic_index_in_dim(tile_stations, my_pair, 0, keepdims=False)
    tile_owner = station_owner[my_tile]
    pooled, pooled_station, pooled_window = (
        lax.all_gather(whitened, "grp", axis=0, tiled=True),
        lax.all_gather(row_station, "grp", axis=0, tiled=True),
        lax.all_gather(row_window, "grp", axis=0, tiled=True),
    )
    wanted = jnp.any(pooled_station[None, :, None] == tile_stations[:, None, :], axis=2)
    wanted = wanted.reshape(pair_groups, group_count, 1, local_count)
    window_hit = (
        pooled_window.reshape(group_count, local_count)[:, None, :] == window_ids[None, :, None]
    )[None]
    selected = wanted & window_hit
    position = jnp.sum(jnp.where(selected, local_ids, 0), axis=3)
    position = position + (jnp.arange(group_count, dtype=jnp.int32) * local_count)[None, :, None]
    present = jnp.any(selected, axis=3)
    outgoing = jnp.where(present.reshape(-1, 1, 1), pooled[position.reshape(-1)], zero_value)
    outgoing = outgoing.reshape((pair_groups, group_count * W) + row_tail)
    arrived = lax.all_to_all(outgoing, "pairs", split_axis=0, concat_axis=0, tiled=True)
    source_rows = arrived.reshape((-1,) + row_tail)
    row_base = tile_owner * W
    pair_lists = pair_index.reshape(2, -1)
    first_rows = row_base[pair_lists[0]][:, None] + window_ids[None, :]
    second_rows = row_base[pair_lists[1]][:, None] + window_ids[None, :]
    running = correlate(source_rows, first_rows, second_rows)
    return running.reshape((pair_index.shape[0], pair_index.shape[1], pair_index.shape[3], LAGS))


def solution(mesh):
    placed = (
        P(("pairs", "grp"), None, None),
        P(("pairs", "grp")),
        P(("pairs", "grp")),
        P(),
        P(),
        P("pairs", "grp", None, None),
    )
    return jax.shard_map(
        on_device,
        mesh=mesh,
        in_specs=placed,
        out_specs=P("pairs", "grp", None, None),
        check_vma=False,
    )
```

profile of v0, /device:TPU:38, one launch (start us, length us, event | category | flops | bytes accessed | tf_op | source)
XLA Modules:
  0.0 268.8 jit_solution(16281639147075482824)
XLA Ops:
  0.0 0.0 copy-start
  0.0 1.3 dynamic-slice
  1.9 0.9 dynamic-update-slice.1
  2.8 0.8 dynamic-update-slice
  3.6 9.5 %all-reduce.2 = (s32[128]{0:T(128)S(1)}, s32[128]{0:T(128)S(1)}) all-reduce(s32[128]{0:T(128)S(1)} %dynamic-update-slice.1, s32[128]{0:T(128)S(1)} %dynamic-update-slice), channel_id=1, replica_groups=mesh['pairs'=64,'grp'=8] {'grp'}, use_global_device_ids=true, to_apply=%add.1 | all-reduce | flops 256 | bytes 2048
  13.1 0.1 eq.38
  13.2 2.1 compare_reduce_fusion
  15.3 0.1 copy.16
  15.5 0.1 and_reduce_fusion
  15.6 0.1 fusion.32
  15.7 0.1 copy.17
  15.9 0.9 fusion.30
  16.7 0.1 reduce_sum.58
  16.9 0.1 mul.188
  17.0 0.9 fusion.31
  17.8 0.1 copy_add_fusion
  17.9 0.2 copy.19
  18.1 0.2 add.216
  18.3 13.1 %all_gather.11 = bf16[128,1,2048]{2,0,1:T(8,128)(2,1)S(1)} all-gather(bf16[16,1,2048]{2,0,1:T(8,128)(2,1)S(1)} %fusion.31), channel_id=1, replica_groups=mesh['pairs'=64,'grp'=8] {'grp'}, dimensions={0}, use_global_device_ids=true | all-gather | bytes 589824 | tf_op jit(solution)/shard_map/all_gather | solution.py:72
  31.4 6.0 %gather_fusion = bf16[1024,2048]{1,0:T(8,128)(2,1)} fusion(bf16[128,2048]{1,0:T(8,128)(2,1)S(1)} %bitcast.42, s32[1024]{0:T(1024)S(1)} %broadcast_clamp_fusion), kind=kCustom, calls=%fused_computation | custom fusion | bytes 8392704 | tf_op jit(solution)/shard_map/gather | solution.py:85
  37.4 4.5 %broadcast_select_fusion = bf16[64,16,1,2048]{3,1,2,0:T(8,128)(2,1)} fusion(bf16[64,16,1,2048]{3,1,2,0:T(8,128)(2,1)} %bitcast.43, pred[64,16]{1,0:T(8,128)(4,1)S(1)} %copy.17), kind=kLoop, calls=%fused_computation.42 | loop fusion | flops 2097152 | bytes 8389632 | tf_op jit(solution)/shard_map/jit(_where)/select_n | solution.py:85
  41.9 0.0 copy-start.3
  42.0 18.7 %all-to-all-start = ((bf16[64,16,1,2048]{3,1,2,0:T(8,128)(2,1)}), bf16[64,16,1,2048]{3,1,2,0:T(8,128)(2,1)}, u32[]{:S(2)}, u32[]{:S(2)}) async-start(bf16[64,16,1,2048]{3,1,2,0:T(8,128)(2,1)} %broadcast_select_fusion), calls=%async_computation | async-start | bytes 8388608 | tf_op jit(solution)/shard_map/all_to_all | solution.py:87
  60.6 0.7 fusion.39
  61.4 0.0 copy-done
  61.4 2.5 gather_fusion.1
  63.9 0.0 copy-done.3
  64.0 0.8 gather_fusion.4
  64.8 0.8 gather_fusion.2
  65.6 0.1 compare_select_fusion.1
  65.7 0.1 reshape.431
  65.8 0.1 compare_select_fusion
  65.9 0.1 reshape.449
  66.0 36.1 %cosine_convert_fusion = (bf16[512,2001]{1,0:T(8,128)(2,1)}, bf16[512,2001]{1,0:T(8,128)(2,1)}, bf16[512,2001]{1,0:T(8,128)(2,1)}, bf16[512,2001]{1,0:T(8,128)(2,1)}) fusion(s32[2001]{0:T(1024)S(1)} %iota_add_fusion, s32[512]{0:T(512)S(1)} %iota_add_fusion.1), kind=kLoop, calls=%fused_computation.36 | loop fusion | flops 34833408 | bytes 8206148 | tf_op jit(solution)/shard_map/convert
  102.1 146.1 %all-to-all-done = bf16[64,16,1,2048]{3,1,2,0:T(8,128)(2,1)} async-done(((bf16[64,16,1,2048]{3,1,2,0:T(8,128)(2,1)}), bf16[64,16,1,2048]{3,1,2,0:T(8,128)(2,1)}, u32[]{:S(2)}, u32[]{:S(2)}) %all-to-all-start) | async-done | bytes 4194336 | tf_op jit(solution)/shard_map/all_to_all | solution.py:87
  248.2 3.6 %slice_bitcast_fusion = (bf16[1024,512]{1,0:T(8,128)(2,1)}, bf16[1024,512]{1,0:T(8,128)(2,1)S(1)}, bf16[1024,512]{1,0:T(8,128)(2,1)S(1)}, bf16[1024,512]{1,0:T(8,128)(2,1)S(1)}) fusion(bf16[1024,1,2048]{2,0,1:T(8,128)(2,1)} %bitcast.6), kind=kLoop, calls=%fused_computation.46 | loop fusion | bytes 8388608 | tf_op jit(solution)/shard_map/slice | solution.py:37
  251.8 2.2 gather_fusion.11
  254.0 2.2 gather_fusion.10
  256.1 0.8 gather_fusion.9
  256.9 1.4 gather_fusion.8
  258.3 0.8 gather_fusion.7
  259.1 0.8 gather_fusion.6
  259.9 0.8 gather_fusion.3
  260.6 0.8 gather_fusion.5
  261.4 1.0 fusion.28
  262.4 0.1 reshape.562
  262.5 0.2 reduce_sum.62
  262.7 0.1 fusion.26
  262.8 0.1 reshape.560
  262.9 0.0 copy-start.1
  262.9 0.2 reduce_sum.60
  263.2 0.1 reshape.561
  263.3 0.2 reduce_sum.61
  263.6 0.1 reshape.563
  263.7 0.2 reduce_sum.63
  263.9 0.0 copy-start.2
  263.9 3.2 %fusion.6 = f32[48,2001]{1,0:T(8,128)S(1)} fusion(bf16[512,2001]{1,0:T(8,128)(2,1)} %get-tuple-element.17, bf16[512,2001]{1,0:T(8,128)(2,1)} %get-tuple-element.18, bf16[48,512]{1,0:T(8,128)(2,1)S(1)} %reduce_sum.61, bf16[48,512]{1,0:T(8,128)(2,1)S(1)} %reduce_sum.60), kind=kOutput, calls=%fused_computation.27 | convolution fusion | flops 205099008 | bytes 4580544 | tf_op jit(solution)/shard_map/dot_general | solution.py:53
  267.1 0.0 copy-done.1
  267.2 0.0 copy-done.2
  267.2 1.6 fusion.23
  (18 shorter events, 0.2 us)
Async XLA Ops:
  0.0 61.4 %copy-start = (s32[4096]{0:T(1024)S(1)}, s32[4096]{0:T(1024)}, u32[]{:S(2)}) copy-start(s32[4096]{0:T(1024)} %param.9) | copy-start | bytes 49156
  41.9 22.0 %copy-start.3 = (s32[1,1,2,48]{3,2,1,0:T(2,128)S(1)}, s32[1,1,2,48]{3,2,1,0:T(2,128)}, u32[]{:S(2)}) copy-start(s32[1,1,2,48]{3,2,1,0:T(2,128)} %param.11) | copy-start | bytes 1156
  42.0 206.2 %all-to-all-start = ((bf16[64,16,1,2048]{3,1,2,0:T(8,128)(2,1)}), bf16[64,16,1,2048]{3,1,2,0:T(8,128)(2,1)}, u32[]{:S(2)}, u32[]{:S(2)}) async-start(bf16[64,16,1,2048]{3,1,2,0:T(8,128)(2,1)} %broadcast_select_fusion), calls=%async_computation | async-start | bytes 8388608 | tf_op jit(solution)/shard_map/all_to_all | solution.py:87
  262.9 4.2 %copy-start.1 = (bf16[512,2001]{1,0:T(8,128)(2,1)S(1)}, bf16[512,2001]{1,0:T(8,128)(2,1)}, u32[]{:S(2)}) copy-start(bf16[512,2001]{1,0:T(8,128)(2,1)} %get-tuple-element.15) | copy-start | bytes 6147076
  263.9 3.2 %copy-start.2 = (bf16[512,2001]{1,0:T(8,128)(2,1)S(1)}, bf16[512,2001]{1,0:T(8,128)(2,1)}, u32[]{:S(2)}) copy-start(bf16[512,2001]{1,0:T(8,128)(2,1)} %get-tuple-element.16) | copy-start | bytes 6147076
where the time goes:
time: 269 us
  waiting for transfers between devices  146 us (54%)
  other arithmetic  47.8 us (18%)
  local copies, waits for them, and re-layouts  27.8 us (10%)
  blocking collectives  22.6 us (8%)
  starting transfers between devices  18.7 us (7%)
  matrix products  4.81 us (2%)
    all_to_all x1, waiting for transfers between devices, on_device(): lax.all_to_all(outgoing, 'pairs', split_axis=0, concat_axis=0, tiled=True)  146 us
    another operation x1, other arithmetic  36.1 us
    all_to_all x1, starting transfers between devices, on_device(): lax.all_to_all(outgoing, 'pairs', split_axis=0, concat_axis=0, tiled=True)  18.7 us
    all_gather x1, blocking collectives, on_device(): lax.all_gather(whitened, 'grp', axis=0, tiled=True)  13.1 us
    unnamed x1, blocking collectives  9.48 us
    gather x1, local copies, waits for them, and re-layouts, on_device(): pooled[position.reshape(-1)]  6.01 us
  transfers between devices with their start and end apart: 1, of which 1 were waited for; matrix products, arithmetic and copies ran while one was open for 15% of the time, Pallas kernels for 0%

commit v1 on v0

--- a/solution.py
+++ b/solution.py
@@ -69,7 +69,9 @@
     my_tile = lax.dynamic_index_in_dim(tile_stations, my_pair, 0, keepdims=False)
     tile_owner = station_owner[my_tile]
     pooled, pooled_station, pooled_window = (
-        lax.all_gather(whitened, "grp", axis=0, tiled=True),
+        jnp.concatenate(
+            lax.all_to_all(jnp.stack([whitened] * lax.axis_size("grp")), "grp", 0, 0), axis=0
+        ),
         lax.all_gather(row_station, "grp", axis=0, tiled=True),
         lax.all_gather(row_window, "grp", axis=0, tiled=True),
     )

time: 269 us -> 261 us (0.970)
  blocking collectives: 22.6 us -> 9.68 us
  starting transfers between devices: 18.7 us -> 23.1 us
    all_gather x1 -> x0, blocking collectives: 13.1 us -> none  [on_device(): lax.all_gather(whitened, 'grp', axis=0, tiled=True)]
    all_to_all x0 -> x1, starting transfers between devices: none -> 4.47 us  [on_device(): lax.all_to_all(jnp.stack([whitened] * lax.axis_size('grp')), 'grp', 0, 0)]
  transfers between devices with their start and end apart: 1 -> 2, of which waited for: 1 -> 1; matrix products, arithmetic and copies ran while one was open for 15% -> 18% of each run, Pallas kernels for 0% -> 0%
where the time goes in v1:
time: 261 us; the launch traced here: 260 us
  waiting for transfers between devices  145 us (56%)
  other arithmetic  47.8 us (18%)
  local copies, waits for them, and re-layouts  28.7 us (11%)
  starting transfers between devices  23.1 us (9%)
  blocking collectives  9.68 us (4%)
  matrix products  4.81 us (2%)
    all_to_all x1, waiting for transfers between devices, on_device(): lax.all_to_all(outgoing, 'pairs', split_axis=0, concat_axis=0, tiled=True)  145 us
    another operation x1, other arithmetic  36.1 us
    all_to_all x1, starting transfers between devices, on_device(): lax.all_to_all(outgoing, 'pairs', split_axis=0, concat_axis=0, tiled=True)  18.7 us
    unnamed x1, blocking collectives  9.68 us
    gather x1, local copies, waits for them, and re-layouts, on_device(): pooled[position.reshape(-1)]  6.02 us
  transfers between devices with their start and end apart: 2, of which 1 were waited for; matrix products, arithmetic and copies ran while one was open for 18% of the time, Pallas kernels for 0%

profile of v1, /device:TPU:38, one launch (start us, length us, event | category | flops | bytes accessed | tf_op | source)
XLA Modules:
  0.0 259.9 jit_solution(1726767515860877633)
XLA Ops:
  0.0 0.0 copy-start
  0.0 0.9 fusion.30
  0.9 0.1 reduce_sum.58
  1.0 0.1 mul.188
  1.1 0.9 fusion.39
  2.0 0.8 stack.2
  2.8 4.5 %all-to-all-start = ((bf16[8,16,1,2048]{3,1,2,0:T(8,128)(2,1)}), bf16[8,16,1,2048]{3,1,2,0:T(8,128)(2,1)S(1)}, u32[]{:S(2)}, u32[]{:S(2)}) async-start(bf16[8,16,1,2048]{3,1,2,0:T(8,128)(2,1)} %stack.2), calls=%async_computation | async-start | bytes 1048576 | tf_op jit(solution)/shard_map/all_to_all | solution.py:73
  7.3 1.3 dynamic-slice
  9.3 0.9 dynamic-update-slice.1
  10.1 0.8 dynamic-update-slice
  11.0 9.7 %all-reduce.2 = (s32[128]{0:T(128)S(1)}, s32[128]{0:T(128)S(1)}) all-reduce(s32[128]{0:T(128)S(1)} %dynamic-update-slice.1, s32[128]{0:T(128)S(1)} %dynamic-update-slice), channel_id=1, replica_groups=mesh['pairs'=64,'grp'=8] {'grp'}, use_global_device_ids=true, to_apply=%add.1 | all-reduce | flops 256 | bytes 2048
  20.6 0.1 eq.38
  20.7 2.1 compare_reduce_fusion
  22.9 0.1 copy.16
  23.0 0.1 fusion.32
  23.1 0.1 copy_add_fusion
  23.2 0.1 and_reduce_fusion
  23.3 0.1 copy.17
  23.4 0.2 copy.19
  23.6 0.2 add.216
  23.8 0.0 all-to-all-done
  23.9 6.0 %gather_fusion = bf16[1024,2048]{1,0:T(8,128)(2,1)} fusion(bf16[128,2048]{1,0:T(8,128)(2,1)S(1)} %bitcast.44, s32[1024]{0:T(1024)S(1)} %broadcast_clamp_fusion), kind=kCustom, calls=%fused_computation | custom fusion | bytes 8392704 | tf_op jit(solution)/shard_map/gather | solution.py:87
  29.9 4.5 %broadcast_select_fusion = bf16[64,16,1,2048]{3,1,2,0:T(8,128)(2,1)} fusion(bf16[64,16,1,2048]{3,1,2,0:T(8,128)(2,1)} %bitcast.45, pred[64,16]{1,0:T(8,128)(4,1)S(1)} %copy.17), kind=kLoop, calls=%fused_computation.42 | loop fusion | flops 2097152 | bytes 8389632 | tf_op jit(solution)/shard_map/jit(_where)/select_n | solution.py:87
  34.4 0.0 copy-start.3
  34.4 18.7 %all-to-all-start.1 = ((bf16[64,16,1,2048]{3,1,2,0:T(8,128)(2,1)}), bf16[64,16,1,2048]{3,1,2,0:T(8,128)(2,1)}, u32[]{:S(2)}, u32[]{:S(2)}) async-start(bf16[64,16,1,2048]{3,1,2,0:T(8,128)(2,1)} %broadcast_select_fusion), calls=%async_computation.1 | async-start | bytes 8388608 | tf_op jit(solution)/shard_map/all_to_all | solution.py:89
  53.1 0.7 fusion.40
  53.8 0.0 copy-done
  53.8 2.5 gather_fusion.1
  56.4 0.0 copy-done.3
  56.4 0.8 gather_fusion.4
  57.2 0.8 gather_fusion.2
  58.0 0.1 compare_select_fusion.1
  58.1 0.1 reshape.438
  58.2 0.1 compare_select_fusion
  58.3 0.1 reshape.456
  58.5 36.1 %cosine_convert_fusion = (bf16[512,2001]{1,0:T(8,128)(2,1)}, bf16[512,2001]{1,0:T(8,128)(2,1)}, bf16[512,2001]{1,0:T(8,128)(2,1)}, bf16[512,2001]{1,0:T(8,128)(2,1)}) fusion(s32[2001]{0:T(1024)S(1)} %iota_add_fusion, s32[512]{0:T(512)S(1)} %iota_add_fusion.1), kind=kLoop, calls=%fused_computation.36 | loop fusion | flops 34833408 | bytes 8206148 | tf_op jit(solution)/shard_map/convert
  94.6 144.8 %all-to-all-done.1 = bf16[64,16,1,2048]{3,1,2,0:T(8,128)(2,1)} async-done(((bf16[64,16,1,2048]{3,1,2,0:T(8,128)(2,1)}), bf16[64,16,1,2048]{3,1,2,0:T(8,128)(2,1)}, u32[]{:S(2)}, u32[]{:S(2)}) %all-to-all-start.1) | async-done | bytes 4194336 | tf_op jit(solution)/shard_map/all_to_all | solution.py:89
  239.3 3.6 %slice_bitcast_fusion = (bf16[1024,512]{1,0:T(8,128)(2,1)}, bf16[1024,512]{1,0:T(8,128)(2,1)S(1)}, bf16[1024,512]{1,0:T(8,128)(2,1)S(1)}, bf16[1024,512]{1,0:T(8,128)(2,1)S(1)}) fusion(bf16[1024,1,2048]{2,0,1:T(8,128)(2,1)} %bitcast.7), kind=kLoop, calls=%fused_computation.46 | loop fusion | bytes 8388608 | tf_op jit(solution)/shard_map/slice | solution.py:37
  242.9 2.2 gather_fusion.11
  245.1 2.2 gather_fusion.10
  247.3 0.8 gather_fusion.9
  248.0 1.4 gather_fusion.8
  249.5 0.8 gather_fusion.7
  250.2 0.8 gather_fusion.6
  251.0 0.8 gather_fusion.3
  251.8 0.8 gather_fusion.5
  252.6 1.0 fusion.28
  253.5 0.1 reshape.570
  253.6 0.2 reduce_sum.62
  253.9 0.1 fusion.26
  254.0 0.1 reshape.568
  254.1 0.0 copy-start.1
  254.1 0.2 reduce_sum.60
  254.3 0.1 reshape.569
  254.5 0.2 reduce_sum.61
  254.7 0.1 reshape.571
  254.8 0.2 reduce_sum.63
  255.1 0.0 copy-start.2
  255.1 3.2 %fusion.6 = f32[48,2001]{1,0:T(8,128)S(1)} fusion(bf16[512,2001]{1,0:T(8,128)(2,1)} %get-tuple-element.17, bf16[512,2001]{1,0:T(8,128)(2,1)} %get-tuple-element.18, bf16[48,512]{1,0:T(8,128)(2,1)S(1)} %reduce_sum.61, bf16[48,512]{1,0:T(8,128)(2,1)S(1)} %reduce_sum.60), kind=kOutput, calls=%fused_computation.27 | convolution fusion | flops 205099008 | bytes 4580544 | tf_op jit(solution)/shard_map/dot_general | solution.py:53
  258.3 0.0 copy-done.1
  258.3 0.0 copy-done.2
  258.3 1.6 fusion.23
  (18 shorter events, 0.2 us)
Async XLA Ops:
  0.0 53.8 %copy-start = (s32[4096]{0:T(1024)S(1)}, s32[4096]{0:T(1024)}, u32[]{:S(2)}) copy-start(s32[4096]{0:T(1024)} %param.9) | copy-start | bytes 49156
  2.8 21.0 %all-to-all-start = ((bf16[8,16,1,2048]{3,1,2,0:T(8,128)(2,1)}), bf16[8,16,1,2048]{3,1,2,0:T(8,128)(2,1)S(1)}, u32[]{:S(2)}, u32[]{:S(2)}) async-start(bf16[8,16,1,2048]{3,1,2,0:T(8,128)(2,1)} %stack.2), calls=%async_computation | async-start | bytes 1048576 | tf_op jit(solution)/shard_map/all_to_all | solution.py:73
  34.4 22.0 %copy-start.3 = (s32[1,1,2,48]{3,2,1,0:T(2,128)S(1)}, s32[1,1,2,48]{3,2,1,0:T(2,128)}, u32[]{:S(2)}) copy-start(s32[1,1,2,48]{3,2,1,0:T(2,128)} %param.11) | copy-start | bytes 1156
  34.4 204.9 %all-to-all-start.1 = ((bf16[64,16,1,2048]{3,1,2,0:T(8,128)(2,1)}), bf16[64,16,1,2048]{3,1,2,0:T(8,128)(2,1)}, u32[]{:S(2)}, u32[]{:S(2)}) async-start(bf16[64,16,1,2048]{3,1,2,0:T(8,128)(2,1)} %broadcast_select_fusion), calls=%async_computation.1 | async-start | bytes 8388608 | tf_op jit(solution)/shard_map/all_to_all | solution.py:89
  254.1 4.2 %copy-start.1 = (bf16[512,2001]{1,0:T(8,128)(2,1)S(1)}, bf16[512,2001]{1,0:T(8,128)(2,1)}, u32[]{:S(2)}) copy-start(bf16[512,2001]{1,0:T(8,128)(2,1)} %get-tuple-element.15) | copy-start | bytes 6147076
  255.1 3.2 %copy-start.2 = (bf16[512,2001]{1,0:T(8,128)(2,1)S(1)}, bf16[512,2001]{1,0:T(8,128)(2,1)}, u32[]{:S(2)}) copy-start(bf16[512,2001]{1,0:T(8,128)(2,1)} %get-tuple-element.16) | copy-start | bytes 6147076
